TPU v7x, 32 devices: a whole 2x2x4 slice. The times are simulated.
32 devices in a mesh: groups: 2 (over x), tok: 16 (over z, y, core).
Axes of the slice: x: 2, y: 2, z: 4, core: 2. Of those that a mesh axis runs over, the one named last changes fastest.
Arguments:
- query_tokens: bfloat16 [3, 4096, 1024], P(None, ('groups', 'tok')), parts along dimension 1, may hold values from -6 to 6
- key_tokens: bfloat16 [3, 4096, 1024], P(None, ('groups', 'tok')), parts along dimension 1, may hold values from -6 to 6
- value_tokens: bfloat16 [3, 4096, 1024], P(None, ('groups', 'tok')), parts along dimension 1, may hold values from -6 to 6
- learn_rates: float32 [3, 4096, 2], P(None, ('groups', 'tok')), parts along dimension 1, may hold values from 0.0009765625 to 0.00390625
- fast_first: bfloat16 [2, 512, 512], P(None, 'tok'), may hold values from -0.25 to 0.25
- fast_third: bfloat16 [2, 512, 512], P(None, 'tok'), may hold values from -0.25 to 0.25
- fast_second: bfloat16 [2, 512, 512], P(None, 'tok'), may hold values from -0.25 to 0.25
- momentum_decay: float32 [2], replicated, may hold values from 0.3 to 0.95
Outputs:
- readout: bfloat16 [3, 4096, 1024], P(None, ('groups', 'tok')), parts along dimension 1
There are 2 independent parts, one for each index of `groups`. A program takes and returns all parts, laid end to end along the dimension named above; an argument that names none is the same for every part. Nothing has to cross between parts.
All inputs are finite; a program needn't handle non-finite values.
Results may differ from a plain program's by a relative error of at most 0.0089.
Values may be sent and summed in bfloat16 or wider, within the bound.
A program may use at most 64 MiB of HBM per device.

v0:
```python
import jax
import jax.numpy as jnp
from jax import lax
from jax.sharding import PartitionSpec as P


def forward_parts(weights, inputs):
    first, third, second = weights
    length = inputs.shape[0]
    head_count = first.shape[0]
    shaped = inputs.reshape(length, head_count, -1)
    pre_gate = jnp.einsum("thd,hfd->htf", shaped, first, preferred_element_type=jnp.float32)
    pre_up = jnp.einsum("thd,hfd->htf", shaped, third, preferred_element_type=jnp.float32)
    hidden = (jax.nn.silu(pre_gate) * pre_up).astype(jnp.bfloat16)
    return (shaped, pre_gate, pre_up, hidden)


def apply_block(weights, inputs):
    shaped, pre_gate, pre_up, hidden = forward_parts(weights, inputs)
    result = jnp.einsum("htf,hdf->thd", hidden, weights[2], preferred_element_type=jnp.float32)
    return result.reshape(inputs.shape[0], -1).astype(jnp.bfloat16)


def partial_steps(weights, keys, values, rates):
    shaped, pre_gate, pre_up, hidden = forward_parts(weights, keys)
    length = keys.shape[0]
    head_count = weights[0].shape[0]
    scaled = (
        rates[:, :, None] * values.reshape(length, head_count, -1).astype(jnp.float32)
    ).astype(jnp.bfloat16)
    step_second = jnp.einsum("thd,htf->hdf", scaled, hidden, preferred_element_type=jnp.float32)
    back = jnp.einsum("thd,hdf->htf", scaled, weights[2], preferred_element_type=jnp.float32)
    sig_gate = jax.nn.sigmoid(pre_gate)
    d_gate = (back * pre_up * sig_gate * (1.0 + pre_gate * (1.0 - sig_gate))).astype(jnp.bfloat16)
    d_up = (back * pre_gate * sig_gate).astype(jnp.bfloat16)
    step_first = jnp.einsum("htf,thd->hfd", d_gate, shaped, preferred_element_type=jnp.float32)
    step_third = jnp.einsum("htf,thd->hfd", d_up, shaped, preferred_element_type=jnp.float32)
    return (step_first, step_third, step_second)


def summed_steps(terms):
    return (
        lax.psum_scatter(terms[0], "tok", scatter_dimension=1, tiled=True),
        lax.psum_scatter(terms[1], "tok", scatter_dimension=1, tiled=True),
        lax.psum_scatter(terms[2], "tok", scatter_dimension=1, tiled=True),
    )


def renorm(old, moved):
    old_norm = jnp.sqrt(jnp.sum(old * old, axis=-1, keepdims=True) + 1e-06)
    moved_norm = jnp.sqrt(jnp.sum(moved * moved, axis=-1, keepdims=True) + 1e-06)
    return moved * old_norm / moved_norm


def full_steps(owned):
    return (
        lax.all_gather(owned[0], "tok", axis=1, tiled=True),
        lax.all_gather(owned[1], "tok", axis=1, tiled=True),
        lax.all_gather(owned[2], "tok", axis=1, tiled=True),
    )


def shards(
    query_tokens,
    key_tokens,
    value_tokens,
    learn_rates,
    fast_first,
    fast_third,
    fast_second,
    momentum_decay,
):
    full_zero = (
        lax.all_gather(fast_first, "tok", axis=1, tiled=True),
        lax.all_gather(fast_third, "tok", axis=1, tiled=True),
        lax.all_gather(fast_second, "tok", axis=1, tiled=True),
    )
    out_zero = apply_block(full_zero, query_tokens[0])
    terms_zero = partial_steps(full_zero, key_tokens[0], value_tokens[0], learn_rates[0])
    terms_one = partial_steps(full_zero, key_tokens[1], value_tokens[1], learn_rates[1])
    step_zero = summed_steps(terms_zero)
    decay = momentum_decay[:, None, None]
    weights_zero = tuple((w.astype(jnp.float32) for w in full_zero))
    whole_zero = full_steps(step_zero)
    weights_one = tuple((renorm(w, w + m) for w, m in zip(weights_zero, whole_zero)))
    full_one = tuple((w.astype(jnp.bfloat16) for w in weights_one))
    out_one = apply_block(full_one, query_tokens[1])
    step_one = summed_steps(terms_one)
    whole_one = full_steps(step_one)
    moment = tuple((decay * m + s for m, s in zip(whole_zero, whole_one)))
    weights_two = tuple((renorm(w, w + m) for w, m in zip(weights_one, moment)))
    full_two = tuple((w.astype(jnp.bfloat16) for w in weights_two))
    out_two = apply_block(full_two, query_tokens[2])
    return jnp.stack([out_zero, out_one, out_two])


def solution(mesh):
    placed = (
        P(None, ("groups", "tok"), None),
        P(None, ("groups", "tok"), None),
        P(None, ("groups", "tok"), None),
        P(None, ("groups", "tok"), None),
        P(None, "tok", None),
        P(None, "tok", None),
        P(None, "tok", None),
        P(),
    )
    return jax.shard_map(
        shards,
        mesh=mesh,
        in_specs=placed,
        out_specs=P(None, ("groups", "tok"), None),
        check_vma=False,
    )
```

profile of v0, /device:TPU:0, one launch (start us, length us, event | category | flops | bytes accessed | tf_op | source)
XLA Modules:
  0.0 798.2 jit_solution(18446105568856472642)
XLA Ops:
  6.5 0.7 all-gather.10.cloned.1.call-update
  7.3 0.7 all-gather.12.cloned.1.call-update
  8.1 0.7 all-gather.14.cloned.1.call-update
  8.8 1.1 fusion.64
  10.6 39.5 %all-gather.10.cloned.1.call-done = bf16[2,512,512]{2,1,0:T(8,128)(2,1)} async-done(((bf16[2,32,512]{2,1,0:T(8,128)(2,1)}), bf16[2,512,512]{2,1,0:T(8,128)(2,1)}) %all-gather.10.cloned.1.call-update) | async-done | bytes 1048592 | tf_op jit(solution)/shard_map/all_gather | solution.py:74
  50.1 1.7 fusion.66
  51.8 37.3 %all-gather.12.cloned.1.call-done = bf16[2,512,512]{2,1,0:T(8,128)(2,1)} async-done(((bf16[2,32,512]{2,1,0:T(8,128)(2,1)}), bf16[2,512,512]{2,1,0:T(8,128)(2,1)}) %all-gather.12.cloned.1.call-update) | async-done | bytes 1048592 | tf_op jit(solution)/shard_map/all_gather | solution.py:75
  89.2 1.7 fusion.67
  90.9 1.9 fusion.33
  92.8 35.4 %all-gather.14.cloned.1.call-done = bf16[2,512,512]{2,1,0:T(8,128)(2,1)} async-done(((bf16[2,32,512]{2,1,0:T(8,128)(2,1)}), bf16[2,512,512]{2,1,0:T(8,128)(2,1)}) %all-gather.14.cloned.1.call-update) | async-done | bytes 1048592 | tf_op jit(solution)/shard_map/all_gather | solution.py:76
  128.2 1.6 fusion.48
  129.8 1.9 fusion.34
  131.8 1.8 fusion.35
  133.9 1.2 reshape.116
  136.9 1.9 fusion.36
  138.9 1.5 fusion.51
  140.4 0.8 copy-done.7
  141.2 1.9 fusion.37
  143.2 3.1 fusion.38
  146.3 46.3 %reduce-scatter.7.cloned.1.call-done = f32[2,32,512]{2,1,0:T(8,128)} async-done(((f32[2,512,512]{2,1,0:T(8,128)}), f32[2,32,512]{2,1,0:T(8,128)}) %reduce-scatter.7.cloned.1.call-update) | async-done | bytes 131088 | tf_op jit(solution)/shard_map/reduce_scatter | solution.py:45
  192.7 64.3 %reduce-scatter.9.cloned.1.call-done = f32[2,32,512]{2,1,0:T(8,128)} async-done(((f32[2,512,512]{2,1,0:T(8,128)}), f32[2,32,512]{2,1,0:T(8,128)}) %reduce-scatter.9.cloned.1.call-update) | async-done | bytes 131088 | tf_op jit(solution)/shard_map/reduce_scatter | solution.py:43
  257.1 64.3 %reduce-scatter.11.cloned.1.call-done = f32[2,32,512]{2,1,0:T(8,128)} async-done(((f32[2,512,512]{2,1,0:T(8,128)}), f32[2,32,512]{2,1,0:T(8,128)}) %reduce-scatter.11.cloned.1.call-update) | async-done | bytes 131088 | tf_op jit(solution)/shard_map/reduce_scatter | solution.py:44
  321.4 64.5 %reduce-scatter.13.cloned.1.call-done = f32[2,32,512]{2,1,0:T(8,128)} async-done(((f32[2,512,512]{2,1,0:T(8,128)}), f32[2,32,512]{2,1,0:T(8,128)}) %reduce-scatter.13.cloned.1.call-update) | async-done | bytes 131088 | tf_op jit(solution)/shard_map/reduce_scatter | solution.py:45
  386.0 64.4 %reduce-scatter.15.cloned.1.call-done = f32[2,32,512]{2,1,0:T(8,128)} async-done(((f32[2,512,512]{2,1,0:T(8,128)}), f32[2,32,512]{2,1,0:T(8,128)}) %reduce-scatter.15.cloned.1.call-update) | async-done | bytes 131088 | tf_op jit(solution)/shard_map/reduce_scatter | solution.py:43
  450.6 64.2 %reduce-scatter.17.cloned.1.call-done = f32[2,32,512]{2,1,0:T(8,128)} async-done(((f32[2,512,512]{2,1,0:T(8,128)}), f32[2,32,512]{2,1,0:T(8,128)}) %reduce-scatter.17.cloned.1.call-update) | async-done | bytes 131088 | tf_op jit(solution)/shard_map/reduce_scatter | solution.py:44
  514.9 2.0 fusion.63
  516.9 1.1 copy.68
  518.0 1.8 copy.70
  519.8 1.8 copy.72
  521.6 1.3 fusion.65
  522.9 2.6 fusion.8
  525.5 1.1 copy.23
  526.6 30.7 %all-gather.16.cloned.1.call-done = f32[2,512,512]{2,1,0:T(8,128)} async-done(((f32[2,32,512]{2,1,0:T(8,128)}), f32[2,512,512]{2,1,0:T(8,128)}) %all-gather.16.cloned.1.call-update) | async-done | bytes 2097168 | tf_op jit(solution)/shard_map/all_gather | solution.py:59
  557.3 2.1 fusion
  559.4 40.3 %all-gather.18.cloned.1.call-done = f32[2,512,512]{2,1,0:T(8,128)} async-done(((f32[2,32,512]{2,1,0:T(8,128)}), f32[2,512,512]{2,1,0:T(8,128)}) %all-gather.18.cloned.1.call-update) | async-done | bytes 2097168 | tf_op jit(solution)/shard_map/all_gather | solution.py:57
  599.7 2.1 fusion.1
  601.9 40.2 %all-gather.20.cloned.1.call-done = f32[2,512,512]{2,1,0:T(8,128)} async-done(((f32[2,32,512]{2,1,0:T(8,128)}), f32[2,512,512]{2,1,0:T(8,128)}) %all-gather.20.cloned.1.call-update) | async-done | bytes 2097168 | tf_op jit(solution)/shard_map/all_gather | solution.py:58
  642.0 2.1 fusion.2
  644.1 40.3 %all-gather.22.cloned.1.call-done = f32[2,512,512]{2,1,0:T(8,128)} async-done(((f32[2,32,512]{2,1,0:T(8,128)}), f32[2,512,512]{2,1,0:T(8,128)}) %all-gather.22.cloned.1.call-update) | async-done | bytes 2097168 | tf_op jit(solution)/shard_map/all_gather | solution.py:59
  684.4 42.3 %all-gather.24.cloned.1.call-done = f32[2,512,512]{2,1,0:T(8,128)} async-done(((f32[2,32,512]{2,1,0:T(8,128)}), f32[2,512,512]{2,1,0:T(8,128)}) %all-gather.24.cloned.1.call-update) | async-done | bytes 2097168 | tf_op jit(solution)/shard_map/all_gather | solution.py:57
  726.7 42.3 %all-gather.26.cloned.1.call-done = f32[2,512,512]{2,1,0:T(8,128)} async-done(((f32[2,32,512]{2,1,0:T(8,128)}), f32[2,512,512]{2,1,0:T(8,128)}) %all-gather.26.cloned.1.call-update) | async-done | bytes 2097168 | tf_op jit(solution)/shard_map/all_gather | solution.py:58
  769.0 7.4 multiply_reduce_fusion
  776.6 1.5 convolution_bitcast_fusion.1
  778.0 4.1 convolution_convert_fusion
  782.2 3.1 convolution_bitcast_fusion.3
  785.3 4.2 convolution_convert_fusion.1
  789.5 1.0 pad_maximum_fusion
  790.6 1.2 copy.48
  (70 shorter events, 3.7 us)
Async XLA Ops:
  6.5 3.5 copy-start.9
  6.5 43.6 %all-gather.10.cloned.1.call-start = ((), (), s32[]{:S(2)}) async-start(), calls=%async_computation.6 | async-start | bytes 1114112 | tf_op jit(solution)/shard_map/all_gather | solution.py:74
  7.3 81.9 %all-gather.12.cloned.1.call-start = ((), (), s32[]{:S(2)}) async-start(), calls=%async_computation.7 | async-start | bytes 1114112 | tf_op jit(solution)/shard_map/all_gather | solution.py:75
  8.0 120.2 %all-gather.14.cloned.1.call-start = ((), (), s32[]{:S(2)}) async-start(), calls=%async_computation.8 | async-start | bytes 1114112 | tf_op jit(solution)/shard_map/all_gather | solution.py:76
  8.7 1.9 copy-start.12
  8.8 183.9 %reduce-scatter.7.cloned.1.call-start = ((), (), s32[]{:S(2)}) async-start(), calls=%async_computation.9 | async-start | bytes 2228224 | tf_op jit(solution)/shard_map/reduce_scatter | solution.py:45
  92.8 164.2 %reduce-scatter.9.cloned.1.call-start = ((), (), s32[]{:S(2)}) async-start(), calls=%async_computation.11 | async-start | bytes 2228224 | tf_op jit(solution)/shard_map/reduce_scatter | solution.py:43
  131.7 189.6 %reduce-scatter.11.cloned.1.call-start = ((), (), s32[]{:S(2)}) async-start(), calls=%async_computation.13 | async-start | bytes 2228224 | tf_op jit(solution)/shard_map/reduce_scatter | solution.py:44
  133.6 1.5 copy-start
  133.6 2.0 copy-start.1
  133.6 252.3 %reduce-scatter.13.cloned.1.call-start = ((), (), s32[]{:S(2)}) async-start(), calls=%async_computation.15 | async-start | bytes 2228224 | tf_op jit(solution)/shard_map/reduce_scatter | solution.py:45
  135.1 1.8 copy-start.8
  135.6 0.8 copy-start.3
  136.1 0.8 copy-start.5
  136.9 2.0 copy-start.2
  138.8 311.6 %reduce-scatter.15.cloned.1.call-start = ((), (), s32[]{:S(2)}) async-start(), calls=%async_computation.17 | async-start | bytes 2228224 | tf_op jit(solution)/shard_map/reduce_scatter | solution.py:43
  138.9 2.3 copy-start.4
  138.9 2.3 copy-start.6
  140.4 0.8 copy-start.7
  143.1 371.7 %reduce-scatter.17.cloned.1.call-start = ((), (), s32[]{:S(2)}) async-start(), calls=%async_computation.19 | async-start | bytes 2228224 | tf_op jit(solution)/shard_map/reduce_scatter | solution.py:44
  146.2 411.1 %all-gather.16.cloned.1.call-start = ((), (), s32[]{:S(2)}) async-start(), calls=%async_computation.10 | async-start | bytes 2228224 | tf_op jit(solution)/shard_map/all_gather | solution.py:59
  192.7 407.1 %all-gather.18.cloned.1.call-start = ((), (), s32[]{:S(2)}) async-start(), calls=%async_computation.12 | async-start | bytes 2228224 | tf_op jit(solution)/shard_map/all_gather | solution.py:57
  257.0 385.0 %all-gather.20.cloned.1.call-start = ((), (), s32[]{:S(2)}) async-start(), calls=%async_computation.14 | async-start | bytes 2228224 | tf_op jit(solution)/shard_map/all_gather | solution.py:58
  321.4 363.1 %all-gather.22.cloned.1.call-start = ((), (), s32[]{:S(2)}) async-start(), calls=%async_computation.16 | async-start | bytes 2228224 | tf_op jit(solution)/shard_map/all_gather | solution.py:59
  385.9 340.8 %all-gather.24.cloned.1.call-start = ((), (), s32[]{:S(2)}) async-start(), calls=%async_computation.18 | async-start | bytes 2228224 | tf_op jit(solution)/shard_map/all_gather | solution.py:57
  450.4 318.6 %all-gather.26.cloned.1.call-start = ((), (), s32[]{:S(2)}) async-start(), calls=%async_computation.20 | async-start | bytes 2228224 | tf_op jit(solution)/shard_map/all_gather | solution.py:58
  601.8 167.2 %copy-start.13 = (f32[2]{0:T(128)S(1)}, f32[2]{0:T(128)}, u32[]{:S(2)}) copy-start(f32[2]{0:T(128)} %param.15) | copy-start | bytes 28
  769.0 7.6 copy-start.10
  785.3 4.2 copy-start.11
Sparse Core Ops, SparseCore 0:
  9.5 40.5 all-gather.9
  52.3 36.8 all-gather.11
  91.4 36.8 all-gather.13
  131.8 60.7 reduce-scatter.6
  196.2 60.7 reduce-scatter.8
  260.6 60.7 reduce-scatter.10
  325.1 60.7 reduce-scatter.12
  389.6 60.7 reduce-scatter.14
  454.1 60.6 reduce-scatter.16
  516.9 40.3 all-gather.15
  559.5 40.1 all-gather.17
  601.8 40.1 all-gather.19
  644.2 40.1 all-gather.21
  686.5 40.1 all-gather.23
  728.7 40.1 all-gather.25
where the time goes:
time: 799 us; the launch traced here: 798 us
  waiting for transfers between devices  719 us (90%)
  matrix products  36.7 us (5%)
  other arithmetic  14.9 us (2%)
  local copies, waits for them, and re-layouts  13.7 us (2%)
  between operations  13.6 us (2%)
    reduce_scatter x2, waiting for transfers between devices, summed_steps(): lax.psum_scatter(terms[0], 'tok', scatter_dimension=1, tiled=True)  129 us
    reduce_scatter x2, waiting for transfers between devices, summed_steps(): lax.psum_scatter(terms[1], 'tok', scatter_dimension=1, tiled=True)  128 us
    reduce_scatter x2, waiting for transfers between devices, summed_steps(): lax.psum_scatter(terms[2], 'tok', scatter_dimension=1, tiled=True)  111 us
    all_gather x2, waiting for transfers between devices, full_steps(): lax.all_gather(owned[0], 'tok', axis=1, tiled=True)  82.6 us
    all_gather x2, waiting for transfers between devices, full_steps(): lax.all_gather(owned[1], 'tok', axis=1, tiled=True)  82.4 us
    all_gather x2, waiting for transfers between devices, full_steps(): lax.all_gather(owned[2], 'tok', axis=1, tiled=True)  71 us
    all_gather x1, waiting for transfers between devices, shards(): lax.all_gather(fast_first, 'tok', axis=1, tiled=True)  39.5 us
    all_gather x1, waiting for transfers between devices, shards(): lax.all_gather(fast_third, 'tok', axis=1, tiled=True)  37.3 us
  transfers between devices with their start and end apart: 15, of which 15 were waited for; matrix products, arithmetic and copies ran while one was open for 5% of the time, Pallas kernels for 0%

commit v1 on v0

--- a/solution.py
+++ b/solution.py
@@ -1,7 +1,40 @@
+import functools
 import jax
 import jax.numpy as jnp
 from jax import lax
 from jax.sharding import PartitionSpec as P
+
+
+def _begin_trees(piece_in, array_dim):
+    piece_in = jnp.moveaxis(piece_in, 0, array_dim)
+    piece_next = piece_in.shape
+    kept_arr = piece_in.reshape(
+        *piece_next[:array_dim],
+        piece_next[array_dim] * piece_next[array_dim + 1],
+        *piece_next[array_dim + 2 :]
+    )
+    return kept_arr
+
+
+def change_the_pools(content, peer_axis):
+    world_n = lax.axis_size(peer_axis)
+    t_next = content[None]
+    for jj in range(world_n.bit_length() - 1):
+        p_next = 1 << jj
+        a_next = tuple(((p, p ^ p_next) for p in range(world_n)))
+        even = lax.ppermute(t_next, peer_axis, a_next)
+        plain = jnp.stack([t_next, even])
+        z1 = lax.axis_index(peer_axis) >> jj & 1
+        t_next = jnp.where(z1 == 0, plain, plain[::-1]).reshape(-1, *content.shape)
+    return t_next
+
+
+def threads_assign(w_in, matrix, dim_at):
+    side_arr = _begin_trees(change_the_pools(w_in, matrix), dim_at)
+    return side_arr
+
+
+_map_ticks = functools.partial(threads_assign, matrix="tok", dim_at=1)
 
 
 def forward_parts(weights, inputs):
@@ -55,7 +88,7 @@
 def full_steps(owned):
     return (
         lax.all_gather(owned[0], "tok", axis=1, tiled=True),
-        lax.all_gather(owned[1], "tok", axis=1, tiled=True),
+        _map_ticks(owned[1]),
         lax.all_gather(owned[2], "tok", axis=1, tiled=True),
     )
 

time: 799 us -> 766 us (0.959)
  waiting for transfers between devices: 719 us -> 661 us
  other arithmetic: 14.9 us -> 28.4 us
  starting transfers between devices: 0.74 us -> 8.73 us
    all_gather x2 -> x0, waiting for transfers between devices: 82.4 us -> none  [full_steps(): lax.all_gather(owned[1], 'tok', axis=1, tiled=True)]
    ppermute x0 -> x8, waiting for transfers between devices: none -> 50.7 us  [change_the_pools(): even = lax.ppermute(t_next, peer_axis, a_next)]
    all_gather x2, waiting for transfers between devices: 71 us -> 59.7 us  [full_steps(): lax.all_gather(owned[2], 'tok', axis=1, tiled=True)]
    another operation x0 -> x10, other arithmetic: none -> 9.87 us  [change_the_pools(): plain = jnp.stack([t_next, even])]
    ppermute x0 -> x8, starting transfers between devices: none -> 8.07 us  [change_the_pools(): even = lax.ppermute(t_next, peer_axis, a_next)]
  transfers between devices with their start and end apart: 15 -> 21, of which waited for: 15 -> 18; matrix products, arithmetic and copies ran while one was open for 5% -> 8% of each run, Pallas kernels for 0% -> 0%
where the time goes in v1:
time: 766 us
  waiting for transfers between devices  661 us (86%)
  matrix products  35.9 us (5%)
  other arithmetic  28.4 us (4%)
  local copies, waits for them, and re-layouts  18 us (2%)
  between operations  13.8 us (2%)
  starting transfers between devices  8.73 us (1%)
    reduce_scatter x2, waiting for transfers between devices, summed_steps(): lax.psum_scatter(terms[1], 'tok', scatter_dimension=1, tiled=True)  125 us
    reduce_scatter x2, waiting for transfers between devices, summed_steps(): lax.psum_scatter(terms[0], 'tok', scatter_dimension=1, tiled=True)  121 us
    reduce_scatter x2, waiting for transfers between devices, summed_steps(): lax.psum_scatter(terms[2], 'tok', scatter_dimension=1, tiled=True)  109 us
    all_gather x2, waiting for transfers between devices, full_steps(): lax.all_gather(owned[0], 'tok', axis=1, tiled=True)  82.4 us
    all_gather x2, waiting for transfers between devices, full_steps(): lax.all_gather(owned[2], 'tok', axis=1, tiled=True)  59.7 us
    ppermute x8, waiting for transfers between devices, change_the_pools(): even = lax.ppermute(t_next, peer_axis, a_next)  50.7 us
    all_gather x1, waiting for transfers between devices, shards(): lax.all_gather(fast_first, 'tok', axis=1, tiled=True)  38.8 us
    all_gather x1, waiting for transfers between devices, shards(): lax.all_gather(fast_third, 'tok', axis=1, tiled=True)  37.3 us
  transfers between devices with their start and end apart: 21, of which 18 were waited for; matrix products, arithmetic and copies ran while one was open for 8% of the time, Pallas kernels for 0%

profile of v1, /device:TPU:0, one launch (start us, length us, event | category | flops | bytes accessed | tf_op | source)
XLA Modules:
  0.0 765.5 jit_solution(2988584175845061346)
XLA Ops:
  8.8 1.8 fusion.70
  11.3 38.8 %all-gather.8.cloned.1.call-done = bf16[2,512,512]{2,1,0:T(8,128)(2,1)} async-done(((bf16[2,32,512]{2,1,0:T(8,128)(2,1)}), bf16[2,512,512]{2,1,0:T(8,128)(2,1)}) %all-gather.8.cloned.1.call-update) | async-done | bytes 1048592 | tf_op jit(solution)/shard_map/all_gather | solution.py:107
  50.1 1.7 fusion.72
  51.9 37.3 %all-gather.10.cloned.1.call-done = bf16[2,512,512]{2,1,0:T(8,128)(2,1)} async-done(((bf16[2,32,512]{2,1,0:T(8,128)(2,1)}), bf16[2,512,512]{2,1,0:T(8,128)(2,1)}) %all-gather.10.cloned.1.call-update) | async-done | bytes 1048592 | tf_op jit(solution)/shard_map/all_gather | solution.py:108
  89.2 1.7 fusion.73
  90.9 1.9 fusion.34
  92.9 35.4 %all-gather.12.cloned.1.call-done = bf16[2,512,512]{2,1,0:T(8,128)(2,1)} async-done(((bf16[2,32,512]{2,1,0:T(8,128)(2,1)}), bf16[2,512,512]{2,1,0:T(8,128)(2,1)}) %all-gather.12.cloned.1.call-update) | async-done | bytes 1048592 | tf_op jit(solution)/shard_map/all_gather | solution.py:109
  128.2 1.6 fusion.53
  130.6 1.8 fusion.35
  135.3 1.9 fusion.37
  137.3 3.2 fusion.36
  140.6 1.5 fusion.56
  142.8 1.9 fusion.39
  144.7 3.3 fusion.38
  148.1 44.5 %reduce-scatter.7.cloned.1.call-done = f32[2,32,512]{2,1,0:T(8,128)} async-done(((f32[2,512,512]{2,1,0:T(8,128)}), f32[2,32,512]{2,1,0:T(8,128)}) %reduce-scatter.7.cloned.1.call-update) | async-done | bytes 131088 | tf_op jit(solution)/shard_map/reduce_scatter | solution.py:78
  192.7 64.3 %reduce-scatter.9.cloned.1.call-done = f32[2,32,512]{2,1,0:T(8,128)} async-done(((f32[2,512,512]{2,1,0:T(8,128)}), f32[2,32,512]{2,1,0:T(8,128)}) %reduce-scatter.9.cloned.1.call-update) | async-done | bytes 131088 | tf_op jit(solution)/shard_map/reduce_scatter | solution.py:76
  257.1 64.3 %reduce-scatter.13.cloned.1.call-done = f32[2,32,512]{2,1,0:T(8,128)} async-done(((f32[2,512,512]{2,1,0:T(8,128)}), f32[2,32,512]{2,1,0:T(8,128)}) %reduce-scatter.13.cloned.1.call-update) | async-done | bytes 131088 | tf_op jit(solution)/shard_map/reduce_scatter | solution.py:78
  321.7 64.3 %reduce-scatter.11.cloned.1.call-done = f32[2,32,512]{2,1,0:T(8,128)} async-done(((f32[2,512,512]{2,1,0:T(8,128)}), f32[2,32,512]{2,1,0:T(8,128)}) %reduce-scatter.11.cloned.1.call-update) | async-done | bytes 131088 | tf_op jit(solution)/shard_map/reduce_scatter | solution.py:77
  385.9 1.6 collective-permute-done
  390.3 60.2 %reduce-scatter.17.cloned.1.call-done = f32[2,32,512]{2,1,0:T(8,128)} async-done(((f32[2,512,512]{2,1,0:T(8,128)}), f32[2,32,512]{2,1,0:T(8,128)}) %reduce-scatter.17.cloned.1.call-update) | async-done | bytes 131088 | tf_op jit(solution)/shard_map/reduce_scatter | solution.py:77
  450.5 1.6 collective-permute-done.4
  457.0 1.5 collective-permute-start.5
  458.4 2.0 fusion.69
  461.6 1.8 copy.82
  463.4 1.8 copy.84
  466.4 2.7 collective-permute-done.2
  469.1 1.3 pad_maximum_fusion.2
  472.6 1.4 collective-permute-start.3
  474.8 1.4 collective-permute-start.6
  477.5 56.6 %reduce-scatter.15.cloned.1.call-done = f32[2,32,512]{2,1,0:T(8,128)} async-done(((f32[2,512,512]{2,1,0:T(8,128)}), f32[2,32,512]{2,1,0:T(8,128)}) %reduce-scatter.15.cloned.1.call-update) | async-done | bytes 131088 | tf_op jit(solution)/shard_map/reduce_scatter | solution.py:76
  534.1 2.6 fusion.9
  537.8 1.3 pad_maximum_fusion.3
  539.4 1.4 collective-permute-start.7
  540.8 1.5 pad_maximum_fusion
  544.0 2.0 multiply_reduce_fusion.1
  546.0 44.8 %collective-permute-done.7 = f32[8,2,32,512]{3,2,0,1:T(8,128)S(1)} collective-permute-done((f32[8,2,32,512]{3,2,0,1:T(8,128)S(1)}, f32[8,2,32,512]{3,2,0,1:T(8,128)S(1)}, u32[]{:S(2)}, u32[]{:S(2)}) %collective-permute-start.7) | collective-permute-done | bytes 1048608 | tf_op jit(solution)/shard_map/ppermute | solution.py:25
  591.0 1.6 reverse_select_fusion
  592.7 19.5 %all-gather.14.cloned.1.call-done = f32[2,512,512]{2,1,0:T(8,128)} async-done(((f32[2,32,512]{2,1,0:T(8,128)}), f32[2,512,512]{2,1,0:T(8,128)}) %all-gather.14.cloned.1.call-update) | async-done | bytes 2097168 | tf_op jit(solution)/shard_map/all_gather | solution.py:92
  612.2 2.4 fusion
  614.6 40.0 %all-gather.16.cloned.1.call-done = f32[2,512,512]{2,1,0:T(8,128)} async-done(((f32[2,32,512]{2,1,0:T(8,128)}), f32[2,512,512]{2,1,0:T(8,128)}) %all-gather.16.cloned.1.call-update) | async-done | bytes 2097168 | tf_op jit(solution)/shard_map/all_gather | solution.py:90
  654.6 2.1 fusion.1
  656.7 40.2 %all-gather.18.cloned.1.call-done = f32[2,512,512]{2,1,0:T(8,128)} async-done(((f32[2,32,512]{2,1,0:T(8,128)}), f32[2,512,512]{2,1,0:T(8,128)}) %all-gather.18.cloned.1.call-update) | async-done | bytes 2097168 | tf_op jit(solution)/shard_map/all_gather | solution.py:92
  696.9 42.4 %all-gather.20.cloned.1.call-done = f32[2,512,512]{2,1,0:T(8,128)} async-done(((f32[2,32,512]{2,1,0:T(8,128)}), f32[2,512,512]{2,1,0:T(8,128)}) %all-gather.20.cloned.1.call-update) | async-done | bytes 2097168 | tf_op jit(solution)/shard_map/all_gather | solution.py:90
  739.3 7.5 multiply_reduce_fusion.4
  747.0 1.5 convolution_bitcast_fusion.1
  748.5 3.5 convolution_convert_fusion
  752.1 2.4 convolution_bitcast_fusion.3
  754.5 3.2 convolution_convert_fusion.1
  (119 shorter events, 26.9 us)
Async XLA Ops:
  6.5 4.2 copy-start.18
  6.5 43.6 %all-gather.8.cloned.1.call-start = ((), (), s32[]{:S(2)}) async-start(), calls=%async_computation.6 | async-start | bytes 1114112 | tf_op jit(solution)/shard_map/all_gather | solution.py:107
  7.3 81.9 %all-gather.10.cloned.1.call-start = ((), (), s32[]{:S(2)}) async-start(), calls=%async_computation.7 | async-start | bytes 1114112 | tf_op jit(solution)/shard_map/all_gather | solution.py:108
  8.0 120.2 %all-gather.12.cloned.1.call-start = ((), (), s32[]{:S(2)}) async-start(), calls=%async_computation.8 | async-start | bytes 1114112 | tf_op jit(solution)/shard_map/all_gather | solution.py:109
  8.7 2.6 copy-start.22
  8.8 183.9 %reduce-scatter.7.cloned.1.call-start = ((), (), s32[]{:S(2)}) async-start(), calls=%async_computation.9 | async-start | bytes 2228224 | tf_op jit(solution)/shard_map/reduce_scatter | solution.py:78
  51.8 78.0 %copy-start.7 = (f32[2,128,512]{2,1,0:T(8,128)}, f32[2,128,512]{2,1,0:T(8,128)S(1)}, u32[]{:S(2)}) copy-start(f32[2,128,512]{2,1,0:T(8,128)S(1)} %fusion.72) | copy-start | bytes 1572868
  92.8 164.2 %reduce-scatter.9.cloned.1.call-start = ((), (), s32[]{:S(2)}) async-start(), calls=%async_computation.11 | async-start | bytes 2228224 | tf_op jit(solution)/shard_map/reduce_scatter | solution.py:76
  129.8 0.8 copy-start.13
  130.6 1.9 copy-start.17
  132.4 1.5 copy-start
  132.5 2.0 copy-start.3
  132.5 188.9 %reduce-scatter.13.cloned.1.call-start = ((), (), s32[]{:S(2)}) async-start(), calls=%async_computation.14 | async-start | bytes 2228224 | tf_op jit(solution)/shard_map/reduce_scatter | solution.py:78
  132.7 2.2 copy-start.10
  134.0 1.3 copy-start.15
  134.5 0.8 copy-start.8
  135.0 2.2 copy-start.12
  137.2 3.3 copy-start.1
  137.2 248.7 %reduce-scatter.11.cloned.1.call-start = ((), (), s32[]{:S(2)}) async-start(), calls=%async_computation.13 | async-start | bytes 2228224 | tf_op jit(solution)/shard_map/reduce_scatter | solution.py:77
  140.5 2.4 copy-start.11
  140.5 310.0 %reduce-scatter.17.cloned.1.call-start = ((), (), s32[]{:S(2)}) async-start(), calls=%async_computation.18 | async-start | bytes 2228224 | tf_op jit(solution)/shard_map/reduce_scatter | solution.py:77
  140.5 2.3 copy-start.9
  142.0 0.8 copy-start.14
  144.7 389.4 %reduce-scatter.15.cloned.1.call-start = ((), (), s32[]{:S(2)}) async-start(), calls=%async_computation.16 | async-start | bytes 2228224 | tf_op jit(solution)/shard_map/reduce_scatter | solution.py:76
  148.1 464.1 %all-gather.14.cloned.1.call-start = ((), (), s32[]{:S(2)}) async-start(), calls=%async_computation.10 | async-start | bytes 2228224 | tf_op jit(solution)/shard_map/all_gather | solution.py:92
  192.7 462.0 %all-gather.16.cloned.1.call-start = ((), (), s32[]{:S(2)}) async-start(), calls=%async_computation.12 | async-start | bytes 2228224 | tf_op jit(solution)/shard_map/all_gather | solution.py:90
  257.0 439.9 %all-gather.18.cloned.1.call-start = ((), (), s32[]{:S(2)}) async-start(), calls=%async_computation.15 | async-start | bytes 2228224 | tf_op jit(solution)/shard_map/all_gather | solution.py:92
  321.4 417.9 %all-gather.20.cloned.1.call-start = ((), (), s32[]{:S(2)}) async-start(), calls=%async_computation.17 | async-start | bytes 2228224 | tf_op jit(solution)/shard_map/all_gather | solution.py:90
  385.9 1.6 collective-permute-start
  389.2 63.8 %collective-permute-start.1 = (f32[2,2,32,512]{3,2,1,0:T(8,128)}, f32[2,2,32,512]{3,2,1,0:T(8,128)}, u32[]{:S(2)}, u32[]{:S(2)}) collective-permute-start(f32[2,2,32,512]{3,2,1,0:T(8,128)} %get-tuple-element.31), channel_id=1, source_target_pairs={{0,2},{1,3},{2,0},{3,1},{4,6},{5,7},{6,4},{7,5},{8,10},{9,11},{10,... | collective-permute-start | bytes 786440 | tf_op jit(solution)/shard_map/ppermute | solution.py:25
  450.5 1.6 collective-permute-start.4
  454.8 14.3 %collective-permute-start.2 = (f32[4,2,32,512]{3,2,1,0:T(8,128)}, f32[4,2,32,512]{3,2,1,0:T(8,128)}, u32[]{:S(2)}, u32[]{:S(2)}) collective-permute-start(f32[4,2,32,512]{3,2,1,0:T(8,128)} %bitcast.15), channel_id=1, source_target_pairs={{0,4},{1,5},{2,6},{3,7},{4,0},{5,1},{6,2},{7,3},{8,12},{9,13},{10,... | collective-permute-start | bytes 1572872 | tf_op jit(solution)/shard_map/ppermute | solution.py:25
  457.0 8.4 %collective-permute-start.5 = (f32[2,2,32,512]{3,2,1,0:T(8,128)}, f32[2,2,32,512]{3,2,1,0:T(8,128)}, u32[]{:S(2)}, u32[]{:S(2)}) collective-permute-start(f32[2,2,32,512]{3,2,1,0:T(8,128)} %get-tuple-element.29), channel_id=1, source_target_pairs={{0,2},{1,3},{2,0},{3,1},{4,6},{5,7},{6,4},{7,5},{8,10},{9,11},{10,... | collective-permute-start | bytes 786440 | tf_op jit(solution)/shard_map/ppermute | solution.py:25
  470.5 1.0 copy-start.5
  472.6 68.2 %collective-permute-start.3 = (f32[8,2,32,512]{3,2,0,1:T(8,128)}, f32[8,2,32,512]{3,2,0,1:T(8,128)}, u32[]{:S(2)}, u32[]{:S(2)}) collective-permute-start(f32[8,2,32,512]{3,2,0,1:T(8,128)} %copy.43), channel_id=1, source_target_pairs={{0,8},{1,9},{2,10},{3,11},{4,12},{5,13},{6,14},{7,15},{8,0},{9,1},... | collective-permute-start | bytes 3145736 | tf_op jit(solution)/shard_map/ppermute | solution.py:25
  474.8 63.0 %collective-permute-start.6 = (f32[4,2,32,512]{3,2,1,0:T(8,128)}, f32[4,2,32,512]{3,2,1,0:T(8,128)}, u32[]{:S(2)}, u32[]{:S(2)}) collective-permute-start(f32[4,2,32,512]{3,2,1,0:T(8,128)} %bitcast.40), channel_id=1, source_target_pairs={{0,4},{1,5},{2,6},{3,7},{4,0},{5,1},{6,2},{7,3},{8,12},{9,13},{10,... | collective-permute-start | bytes 1572872 | tf_op jit(solution)/shard_map/ppermute | solution.py:25
  539.1 1.6 copy-start.6
  539.4 51.4 %collective-permute-start.7 = (f32[8,2,32,512]{3,2,0,1:T(8,128)S(1)}, f32[8,2,32,512]{3,2,0,1:T(8,128)S(1)}, u32[]{:S(2)}, u32[]{:S(2)}) collective-permute-start(f32[8,2,32,512]{3,2,0,1:T(8,128)S(1)} %copy.58), channel_id=1, source_target_pairs={{0,8},{1,9},{2,10},{3,11},{4,12},{5,13},{6,14},{7,15},{8,0},{9,1},... | collective-permute-start | bytes 3145736 | tf_op jit(solution)/shard_map/ppermute | solution.py:25
  542.3 1.3 copy-start.4
  614.6 124.7 %copy-start.23 = (f32[2]{0:T(128)S(1)}, f32[2]{0:T(128)}, u32[]{:S(2)}) copy-start(f32[2]{0:T(128)} %param.15) | copy-start | bytes 28
  739.3 7.6 copy-start.20
  747.0 1.6 copy-start.16
  752.1 2.4 copy-start.2
  752.1 2.4 copy-start.19
  754.5 3.2 copy-start.21
Sparse Core Ops, SparseCore 0:
  9.5 40.5 all-gather.7
  52.3 36.8 all-gather.9
  91.4 36.8 all-gather.11
  131.8 60.7 reduce-scatter.6
  196.2 60.7 reduce-scatter.8
  260.6 60.7 reduce-scatter.12
  325.1 60.7 reduce-scatter.10
  389.7 60.7 reduce-scatter.16
  454.2 79.8 reduce-scatter.14
  536.1 75.9 all-gather.13
  614.4 40.1 all-gather.15
  656.7 40.1 all-gather.17
  699.1 40.1 all-gather.19
